TPU v7x, 512 devices: a whole 4x8x8 slice. The times are simulated.
512 devices in a mesh: rows: 16 (over x, y_lo, core), dp: 32 (over z, y_hi).
Axes of the slice: x: 4, y: 8 (y_hi: 4, y_lo: 2; y = y_hi * 2 + y_lo), z: 8, core: 2. Of those that a mesh axis runs over, the one named last changes fastest.
Arguments:
- images: bfloat16 [32, 32, 512, 128], P('dp', 'rows'), may hold values from -54 to 54
- conv_weight: bfloat16 [3, 3, 128, 128], replicated, may hold values from -0.1875 to 0.1875
- conv_bias: float32 [128], replicated, may hold values from -3 to 3
- norm_gain: float32 [128], replicated, may hold values from 0.5 to 1.5
- norm_shift: float32 [128], replicated, may hold values from -3 to 3
- down_weight: bfloat16 [3, 3, 128, 256], replicated, may hold values from -0.1875 to 0.1875
- down_bias: float32 [256], replicated, may hold values from -3 to 3
- cotangent: bfloat16 [32, 16, 256, 256], P('dp', 'rows'), may hold values from -6 to 6
Outputs:
- block_out: bfloat16 [32, 16, 256, 256], P('dp', 'rows')
- grad_images: bfloat16 [32, 32, 512, 128], P('dp', 'rows')
- grad_conv_weight: float32 [3, 3, 128, 128], P(None, None, None, 'dp')
- grad_conv_bias: float32 [128], P('dp')
- grad_gain: float32 [128], P('dp')
- grad_shift: float32 [128], P('dp')
- grad_down_weight: float32 [3, 3, 128, 256], P(None, None, None, 'dp')
- grad_down_bias: float32 [256], P('dp')
All inputs are finite; a program needn't handle non-finite values.
Results may differ from a plain program's by a relative error of at most 0.0048.
Values may be sent and summed in bfloat16 or wider, within the bound.
A program may use at most 64 MiB of HBM per device.

v0:
```python
import jax
import jax.numpy as jnp
from jax import lax
from jax.sharding import PartitionSpec as P

GROUPS = 32


def extended(block, sides, width):
    for axis, dim in sides:
        count = lax.axis_size(axis)
        forward = [(i, i + 1) for i in range(count - 1)]
        backward = [(target, source) for source, target in forward]
        low = lax.ppermute(
            lax.slice_in_dim(block, block.shape[dim] - width, None, axis=dim), axis, forward
        )
        high = lax.ppermute(lax.slice_in_dim(block, 0, width, axis=dim), axis, backward)
        block = jnp.concatenate([low, block, high], axis=dim)
    return block


def from_behind(x, axis, by):
    length = lax.axis_size(axis)
    pairs = [(i, i + by) for i in range(length) if 0 <= i + by < length]
    return lax.ppermute(x, axis, pairs)


def taps_conv(padded, weight, rows, cols):
    total = jnp.zeros((rows * cols, weight.shape[3]), jnp.float32)
    for kh in range(3):
        for kw in range(3):
            piece = padded[kh : kh + rows, kw : kw + cols].reshape(rows * cols, -1)
            total = total + jnp.dot(piece, weight[kh, kw], preferred_element_type=jnp.float32)
    return total.reshape(rows, cols, weight.shape[3])


def weave(part_zero, part_one, part_two, axis):
    lead = [(0, 0)] * part_zero.ndim
    after = list(lead)
    before = list(lead)
    after[axis] = (0, 1)
    before[axis] = (1, 0)
    even = jnp.pad(part_zero, after) + jnp.pad(part_two, before)
    odd = jnp.pad(part_one, after)
    joined = jnp.stack([even, odd], axis + 1)
    shape = list(even.shape)
    shape[axis] = 2 * shape[axis]
    return joined.reshape(shape)


def shards(
    images, conv_weight, conv_bias, norm_gain, norm_shift, down_weight, down_bias, cotangent
):
    image = images[0]
    cot = cotangent[0]
    rows, cols, chans = image.shape
    half_rows, half_cols, outs = cot.shape
    width = chans // GROUPS
    count = float(rows * cols * width * lax.axis_size("rows"))
    framed = extended(image, (("rows", 0),), 1)
    padded = jnp.pad(framed, ((0, 0), (1, 1), (0, 0)))
    hidden = taps_conv(padded, conv_weight, rows, cols) + conv_bias
    grouped = hidden.reshape(rows, cols, GROUPS, width)
    mean = lax.psum(jnp.sum(grouped, axis=(0, 1, 3)), "rows") / count
    centred = grouped - mean[:, None]
    var = lax.psum(jnp.sum(centred * centred, axis=(0, 1, 3)), "rows") / count
    rstd = lax.rsqrt(var + 1e-05)
    normed = (centred * rstd[:, None]).reshape(rows, cols, chans)
    pre = normed * norm_gain + norm_shift
    sig = jax.nn.sigmoid(pre)
    mixed = (image.astype(jnp.float32) + pre * sig).astype(jnp.bfloat16)
    above = from_behind(mixed[-1], "rows", 1)
    shifted = jnp.pad(jnp.concatenate([above[None], mixed], 0), ((0, 0), (1, 0), (0, 0)))
    cot_flat = cot.reshape(half_rows * half_cols, outs)
    out = jnp.zeros((half_rows * half_cols, outs), jnp.float32)
    grad_down = []
    backs = []
    for kh in range(3):
        line = []
        back_line = []
        for kw in range(3):
            piece = shifted[kh : kh + 2 * half_rows : 2, kw : kw + 2 * half_cols : 2].reshape(
                half_rows * half_cols, chans
            )
            out = out + jnp.dot(piece, down_weight[kh, kw], preferred_element_type=jnp.float32)
            line.append(jnp.dot(piece.T, cot_flat, preferred_element_type=jnp.float32))
            back = jnp.dot(cot_flat, down_weight[kh, kw].T, preferred_element_type=jnp.float32)
            back_line.append(back.reshape(half_rows, half_cols, chans))
        grad_down.append(jnp.stack(line))
        backs.append(weave(back_line[0], back_line[1], back_line[2], 1))
    block = (out + down_bias).astype(jnp.bfloat16).reshape(half_rows, half_cols, outs)
    grad_down = jnp.stack(grad_down)
    grad_down_bias = jnp.sum(cot.astype(jnp.float32), axis=(0, 1))
    woven = weave(backs[0], backs[1], backs[2], 0)
    local_grad = woven[1 : rows + 1, 1 : cols + 1]
    from_below = from_behind(woven[0, 1 : cols + 1], "rows", -1)
    grad_mixed = jnp.concatenate([local_grad[:-1], local_grad[-1:] + from_below[None]], 0)
    grad_pre = grad_mixed * sig * (1.0 + pre * (1.0 - sig))
    grad_gain = jnp.sum(grad_pre * normed, axis=(0, 1))
    grad_shift = jnp.sum(grad_pre, axis=(0, 1))
    scaled = (grad_pre * norm_gain).reshape(rows, cols, GROUPS, width)
    normed_g = normed.reshape(rows, cols, GROUPS, width)
    first, second = lax.psum(
        (jnp.sum(scaled, axis=(0, 1, 3)), jnp.sum(scaled * normed_g, axis=(0, 1, 3))), "rows"
    )
    first = first / count
    second = second / count
    grad_hidden = (rstd[:, None] * (scaled - first[:, None] - normed_g * second[:, None])).reshape(
        rows, cols, chans
    )
    grad_bias = jnp.sum(grad_hidden, axis=(0, 1))
    rounded = grad_hidden.astype(jnp.bfloat16)
    flat = rounded.reshape(rows * cols, chans)
    grad_conv = []
    for kh in range(3):
        line = []
        for kw in range(3):
            piece = padded[kh : kh + rows, kw : kw + cols].reshape(rows * cols, chans)
            line.append(jnp.dot(piece.T, flat, preferred_element_type=jnp.float32))
        grad_conv.append(jnp.stack(line))
    grad_conv = jnp.stack(grad_conv)
    grad_framed = extended(rounded, (("rows", 0),), 1)
    grad_pad = jnp.pad(grad_framed, ((0, 0), (1, 1), (0, 0)))
    back_total = jnp.zeros((rows * cols, chans), jnp.float32)
    for kh in range(3):
        for kw in range(3):
            piece = grad_pad[2 - kh : 2 - kh + rows, 2 - kw : 2 - kw + cols].reshape(
                rows * cols, chans
            )
            back_total = back_total + jnp.dot(
                piece, conv_weight[kh, kw].T, preferred_element_type=jnp.float32
            )
    grad_image = (grad_mixed + back_total.reshape(rows, cols, chans)).astype(jnp.bfloat16)
    conv_pack = grad_conv.reshape(9 * chans, chans)
    small_pack = jnp.stack([grad_bias, grad_gain, grad_shift])
    down_pack = grad_down.reshape(9 * chans, outs)
    bias_pack = grad_down_bias[None]
    count_dp = lax.axis_size("dp")
    totals = lax.psum((conv_pack, small_pack, down_pack, bias_pack), ("rows", "dp"))
    owner = lax.axis_index("dp")
    narrow = chans // count_dp
    wide = outs // count_dp
    conv_part = lax.dynamic_slice_in_dim(totals[0], owner * narrow, narrow, 1)
    small_part = lax.dynamic_slice_in_dim(totals[1], owner * narrow, narrow, 1)
    down_part = lax.dynamic_slice_in_dim(totals[2], owner * wide, wide, 1)
    bias_part = lax.dynamic_slice_in_dim(totals[3], owner * wide, wide, 1)
    return (
        block[None],
        grad_image[None],
        conv_part.reshape(3, 3, chans, -1),
        small_part[0],
        small_part[1],
        small_part[2],
        down_part.reshape(3, 3, chans, -1),
        bias_part[0],
    )


def solution(mesh):
    in_specs = (
        P("dp", "rows", None, None),
        P(),
        P(),
        P(),
        P(),
        P(),
        P(),
        P("dp", "rows", None, None),
    )
    out_specs = (
        P("dp", "rows", None, None),
        P("dp", "rows", None, None),
        P(None, None, None, "dp"),
        P("dp"),
        P("dp"),
        P("dp"),
        P(None, None, None, "dp"),
        P("dp"),
    )
    return jax.shard_map(shards, mesh=mesh, in_specs=in_specs, out_specs=out_specs, check_vma=False)
```

profile of v0, /device:TPU:1, one launch (start us, length us, event | category | flops | bytes accessed | tf_op | source)
XLA Modules:
  0.0 581.2 jit_solution(11627743747505670904)
XLA Ops:
  7.2 1.1 copy.33
  9.1 4.6 collective-permute-start
  13.7 5.5 collective-permute-start.1
  25.5 1.9 collective-permute-start.3
  31.7 1.3 select_maximum_fusion.2
  34.1 1.8 copy.43
  35.9 1.8 copy.41
  41.4 1.2 convolution_add_fusion.15
  46.1 25.3 %psum.56 = f32[32]{0:T(128)S(1)} all-reduce(f32[32]{0:T(128)S(1)} %reduce_sum.83), channel_id=1, replica_groups=mesh['rows'=16,'dp'=32] {'rows'}, use_global_device_ids=true, to_apply=%region_2.3 | all-reduce | flops 32 | bytes 256 | tf_op jit(solution)/shard_map/psum | solution.py:64
  71.9 30.0 %psum.57 = f32[32]{0:T(128)S(1)} all-reduce(f32[32]{0:T(128)S(1)} %reduce_sum.105), channel_id=1, replica_groups=mesh['rows'=16,'dp'=32] {'rows'}, use_global_device_ids=true, to_apply=%region_5.6 | all-reduce | flops 32 | bytes 256 | tf_op jit(solution)/shard_map/psum | solution.py:66
  106.4 27.1 %all-reduce.17 = (f32[32]{0:T(128)S(1)}, f32[32]{0:T(128)S(1)}) all-reduce(f32[32]{0:T(128)S(1)} %reduce_sum.111, f32[32]{0:T(128)S(1)} %reduce_sum.108), channel_id=1, replica_groups=mesh['rows'=16,'dp'=32] {'rows'}, use_global_device_ids=true, to_apply=%region_11.12 | all-reduce | flops 64 | bytes 512 | tf_op jit(solution)/shard_map/psum | solution.py:103
  134.9 1.8 multiply_convert_fusion
  143.0 1.1 fusion.128
  144.4 101.7 %all-reduce.15 = (f32[3,128]{1,0:T(4,128)S(1)}, f32[1,256]{1,0:T(1,128)S(1)}) all-reduce(f32[3,128]{1,0:T(4,128)S(1)} %pad_maximum_fusion.12, f32[1,256]{1,0:T(1,128)S(1)} %bitcast.406), channel_id=1, replica_groups=mesh['rows'=16,'dp'=32] {'rows','dp'}, use_global_device_ids=true, to_apply=%region_16.17 | all-reduce | flops 640 | bytes 5120 | tf_op jit(solution)/shard_map/psum | solution.py:139
  247.6 4.4 collective-permute-start.2
  252.0 1.1 convolution_bitcast_fusion.18
  254.6 2.0 collective-permute-start.4
  256.6 3.0 collective-permute-start.5
  261.4 2.4 slice.255
  263.8 2.4 slice.253
  266.2 2.4 slice.251
  268.5 2.4 slice.249
  270.9 2.4 slice.247
  273.3 2.4 slice.245
  275.6 2.4 slice.243
  278.0 2.4 slice.241
  280.4 2.6 slice.257
  284.9 1.4 copy.71
  289.1 1.3 select_maximum_fusion
  301.1 270.4 %all-reduce.20.cloned.1.call-done = (f32[1152,128]{0,1:T(8,128)}, f32[1152,256]{0,1:T(8,128)}) async-done(((f32[1152,128]{0,1:T(8,128)}, f32[1152,256]{0,1:T(8,128)}), (f32[1152,128]{0,1:T(8,128)}, f32[1152,256]{0,1:T(8,128)})) %all-reduce.20.cloned.1.call-update) | async-done | bytes 1769488 | tf_op jit(solution)/shard_map/psum | solution.py:139
  571.5 1.4 constant_dynamic-slice_fusion.3
  572.9 1.4 constant_dynamic-slice_fusion.1
  (232 shorter events, 51.7 us)
Async XLA Ops:
  7.2 13.1 %copy-start = (bf16[1,1,256,256]{3,2,1,0:T(8,128)(2,1)S(1)}, bf16[1,1,256,256]{3,2,1,0:T(8,128)(2,1)}, u32[]{:S(2)}) copy-start(bf16[1,1,256,256]{3,2,1,0:T(8,128)(2,1)} %param.15) | copy-start | bytes 393220
  7.2 13.1 %copy-start.1 = (bf16[3,3,128,256]{3,2,1,0:T(8,128)(2,1)S(1)}, bf16[3,3,128,256]{3,2,1,0:T(8,128)(2,1)}, u32[]{:S(2)}) copy-start(bf16[3,3,128,256]{3,2,1,0:T(8,128)(2,1)} %param.13) | copy-start | bytes 1769476
  7.2 564.4 %all-reduce.20.cloned.1.call-start = ((), (), s32[]{:S(2)}) async-start(), calls=%async_computation | async-start | bytes 3538944 | tf_op jit(solution)/shard_map/psum | solution.py:139
  9.1 20.0 %collective-permute-start = (bf16[1,512,128]{1,2,0:T(8,128)(2,1)}, bf16[1,512,128]{1,2,0:T(8,128)(2,1)S(1)}, u32[]{:S(2)}, u32[]{:S(2)}) collective-permute-start(bf16[1,512,128]{1,2,0:T(8,128)(2,1)} %get-tuple-element.60), channel_id=1, source_target_pairs={{0,32},{32,64},{64,96},{96,128},{128,160},{160,192},{192,224},{224... | collective-permute-start | bytes 393224 | tf_op jit(solution)/shard_map/ppermute | solution.py:14
  13.7 15.4 %collective-permute-start.1 = (bf16[1,512,128]{1,2,0:T(8,128)(2,1)}, bf16[1,512,128]{1,2,0:T(8,128)(2,1)}, u32[]{:S(2)}, u32[]{:S(2)}) collective-permute-start(bf16[1,512,128]{1,2,0:T(8,128)(2,1)} %get-tuple-element.61), channel_id=1, source_target_pairs={{32,0},{64,32},{96,64},{128,96},{160,128},{192,160},{224,192},{256... | collective-permute-start | bytes 393224 | tf_op jit(solution)/shard_map/ppermute | solution.py:17
  25.5 6.2 %copy-start.5 = (f32[1,512,128]{1,2,0:T(8,128)}, f32[1,512,128]{1,2,0:T(8,128)S(1)}, u32[]{:S(2)}) copy-start(f32[1,512,128]{1,2,0:T(8,128)S(1)} %get-tuple-element.38) | copy-start | bytes 786436
  25.5 77.5 %collective-permute-start.3 = (f32[512,128]{0,1:T(8,128)}, f32[512,128]{0,1:T(8,128)}, u32[]{:S(2)}, u32[]{:S(2)}) collective-permute-start(f32[512,128]{0,1:T(8,128)} %get-tuple-element.37), channel_id=1, source_target_pairs={{32,0},{64,32},{96,64},{128,96},{160,128},{192,160},{224,192},{256... | collective-permute-start | bytes 786440 | tf_op jit(solution)/shard_map/ppermute | solution.py:25
  40.4 2.3 copy-start.9
  40.4 2.3 copy-start.22
  41.4 1.5 copy-start.20
  71.7 32.8 %copy-start.12 = (f32[1,512,32,4]{1,0,3,2:T(1,128)S(1)}, f32[1,512,32,4]{1,0,3,2:T(1,128)}, u32[]{:S(2)}) copy-start(f32[1,512,32,4]{1,0,3,2:T(1,128)} %concatenate.65) | copy-start | bytes 786436
  105.1 29.9 %copy-start.6 = (f32[1,512,128]{1,2,0:T(8,128)S(1)}, f32[1,512,128]{1,2,0:T(8,128)}, u32[]{:S(2)}) copy-start(f32[1,512,128]{1,2,0:T(8,128)} %copy-done.5) | copy-start | bytes 786436
  105.6 29.3 %copy-start.7 = (f32[2,512,128]{1,2,0:T(8,128)S(1)}, f32[2,512,128]{1,2,0:T(8,128)}, u32[]{:S(2)}) copy-start(f32[2,512,128]{1,2,0:T(8,128)} %copy.44) | copy-start | bytes 1572868
  143.0 103.7 %copy-start.4 = (bf16[1,2,512,128]{3,2,1,0:T(8,128)(2,1)S(1)}, bf16[1,2,512,128]{3,2,1,0:T(8,128)(2,1)}, u32[]{:S(2)}) copy-start(bf16[1,2,512,128]{3,2,1,0:T(8,128)(2,1)} %param.8) | copy-start | bytes 786436
  144.1 102.8 %copy-start.8 = (bf16[2,512,128]{1,2,0:T(8,128)(2,1)S(1)}, bf16[2,512,128]{1,2,0:T(8,128)(2,1)}, u32[]{:S(2)}) copy-start(bf16[2,512,128]{1,2,0:T(8,128)(2,1)} %get-tuple-element.52) | copy-start | bytes 786436
  144.1 107.9 %copy-start.35 = (f32[1,128,128]{2,1,0:T(8,128)S(1)}, f32[1,128,128]{2,1,0:T(8,128)}, u32[]{:S(2)}) copy-start(f32[1,128,128]{2,1,0:T(8,128)} %convolution_bitcast_fusion.23) | copy-start | bytes 196612
  144.1 107.9 %copy-start.36 = (f32[1,128,128]{2,1,0:T(8,128)S(1)}, f32[1,128,128]{2,1,0:T(8,128)}, u32[]{:S(2)}) copy-start(f32[1,128,128]{2,1,0:T(8,128)} %convolution_bitcast_fusion.24) | copy-start | bytes 196612
  144.3 108.8 %copy-start.33 = (f32[1,128,128]{2,1,0:T(8,128)S(1)}, f32[1,128,128]{2,1,0:T(8,128)}, u32[]{:S(2)}) copy-start(f32[1,128,128]{2,1,0:T(8,128)} %convolution_bitcast_fusion.22) | copy-start | bytes 196612
  144.3 108.8 %copy-start.34 = (f32[1,128,128]{2,1,0:T(8,128)S(1)}, f32[1,128,128]{2,1,0:T(8,128)}, u32[]{:S(2)}) copy-start(f32[1,128,128]{2,1,0:T(8,128)} %convolution_bitcast_fusion.21) | copy-start | bytes 196612
  247.6 5.8 %copy-start.31 = (f32[1,128,128]{2,1,0:T(8,128)S(1)}, f32[1,128,128]{2,1,0:T(8,128)}, u32[]{:S(2)}) copy-start(f32[1,128,128]{2,1,0:T(8,128)} %convolution_bitcast_fusion.25) | copy-start | bytes 196612
  247.6 5.8 %copy-start.32 = (f32[1,128,128]{2,1,0:T(8,128)S(1)}, f32[1,128,128]{2,1,0:T(8,128)}, u32[]{:S(2)}) copy-start(f32[1,128,128]{2,1,0:T(8,128)} %convolution_bitcast_fusion.26) | copy-start | bytes 196612
  247.6 12.7 %collective-permute-start.2 = (bf16[512,128]{0,1:T(8,128)(2,1)}, bf16[512,128]{0,1:T(8,128)(2,1)}, u32[]{:S(2)}, u32[]{:S(2)}) collective-permute-start(bf16[512,128]{0,1:T(8,128)(2,1)} %slice_bitcast_fusion.1), channel_id=1, source_target_pairs={{0,32},{32,64},{64,96},{96,128},{128,160},{160,192},{192,224},{224... | collective-permute-start | bytes 393224 | tf_op jit(solution)/shard_map/ppermute | solution.py:25
  254.6 28.5 %copy-start.2 = (bf16[3,3,128,256]{3,2,1,0:T(8,128)(2,1)S(1)}, bf16[3,3,128,256]{3,2,1,0:T(8,128)(2,1)}, u32[]{:S(2)}) copy-start(bf16[3,3,128,256]{3,2,1,0:T(8,128)(2,1)} %param.13) | copy-start | bytes 1769476
  254.6 32.4 %collective-permute-start.4 = (bf16[1,512,128]{1,2,0:T(8,128)(2,1)}, bf16[1,512,128]{1,2,0:T(8,128)(2,1)}, u32[]{:S(2)}, u32[]{:S(2)}) collective-permute-start(bf16[1,512,128]{1,2,0:T(8,128)(2,1)} %get-tuple-element.56), channel_id=1, source_target_pairs={{0,32},{32,64},{64,96},{96,128},{128,160},{160,192},{192,224},{224... | collective-permute-start | bytes 393224 | tf_op jit(solution)/shard_map/ppermute | solution.py:14
  256.6 30.4 %collective-permute-start.5 = (bf16[1,512,128]{1,2,0:T(8,128)(2,1)}, bf16[1,512,128]{1,2,0:T(8,128)(2,1)}, u32[]{:S(2)}, u32[]{:S(2)}) collective-permute-start(bf16[1,512,128]{1,2,0:T(8,128)(2,1)} %get-tuple-element.57), channel_id=1, source_target_pairs={{32,0},{64,32},{96,64},{128,96},{160,128},{192,160},{224,192},{256... | collective-permute-start | bytes 393224 | tf_op jit(solution)/shard_map/ppermute | solution.py:17
  266.1 18.2 %copy-start.23 = (bf16[1,256,128]{1,2,0:T(8,128)(2,1)}, bf16[1,256,128]{1,2,0:T(8,128)(2,1)S(1)}, u32[]{:S(2)}) copy-start(bf16[1,256,128]{1,2,0:T(8,128)(2,1)S(1)} %slice.253) | copy-start | bytes 196612
  268.5 15.7 %copy-start.25 = (bf16[1,256,128]{1,2,0:T(8,128)(2,1)}, bf16[1,256,128]{1,2,0:T(8,128)(2,1)S(1)}, u32[]{:S(2)}) copy-start(bf16[1,256,128]{1,2,0:T(8,128)(2,1)S(1)} %slice.251) | copy-start | bytes 196612
  270.9 13.1 %copy-start.27 = (bf16[1,256,128]{1,2,0:T(8,128)(2,1)}, bf16[1,256,128]{1,2,0:T(8,128)(2,1)S(1)}, u32[]{:S(2)}) copy-start(bf16[1,256,128]{1,2,0:T(8,128)(2,1)S(1)} %slice.249) | copy-start | bytes 196612
  291.6 2.2 copy-start.10
  297.7 1.9 copy-start.26
  298.7 1.5 copy-start.30
  298.7 1.5 copy-start.43
  (19 other events, 20.3 us)
Sparse Core Ops, SparseCore 0:
  297.8 273.7 all-reduce.19
where the time goes:
time: 582 us; the launch traced here: 581 us
  waiting for transfers between devices  270 us (46%)
  blocking collectives  184 us (32%)
  local copies, waits for them, and re-layouts  57.4 us (10%)
  starting transfers between devices  21.5 us (4%)
  matrix products  19.1 us (3%)
  between operations  15.3 us (3%)
  other arithmetic  13.4 us (2%)
    psum x1, waiting for transfers between devices, shards(): lax.psum((conv_pack, small_pack, down_pack, bias_pack), ('rows', 'dp'))  270 us
    psum x1, blocking collectives, shards(): lax.psum((conv_pack, small_pack, down_pack, bias_pack), ('rows', 'dp'))  102 us
    psum x1, blocking collectives, shards(): var = lax.psum(jnp.sum(centred * centred, axis=(0, 1, 3)), 'rows') / count  30 us
    psum x1, blocking collectives, shards(): lax.psum((jnp.sum(scaled, axis=(0, 1, 3)), jnp.sum(scaled * normed_g, axi...  27.1 us
    psum x1, blocking collectives, shards(): mean = lax.psum(jnp.sum(grouped, axis=(0, 1, 3)), 'rows') / count  25.3 us
    slice x9, local copies, waits for them, and re-layouts, shards(): shifted[kh:kh + 2 * half_rows:2, kw:kw + 2 * half_cols:2]  21.5 us
  transfers between devices with their start and end apart: 7, of which 1 were waited for; matrix products, arithmetic and copies ran while one was open for 10% of the time, Pallas kernels for 0%

commit v1 on v0

--- a/solution.py
+++ b/solution.py
@@ -63,7 +63,9 @@
     grouped = hidden.reshape(rows, cols, GROUPS, width)
     mean = lax.psum(jnp.sum(grouped, axis=(0, 1, 3)), "rows") / count
     centred = grouped - mean[:, None]
-    var = lax.psum(jnp.sum(centred * centred, axis=(0, 1, 3)), "rows") / count
+    var = (
+        jnp.sum(lax.all_gather(jnp.sum(centred * centred, axis=(0, 1, 3)), "rows"), axis=0) / count
+    )
     rstd = lax.rsqrt(var + 1e-05)
     normed = (centred * rstd[:, None]).reshape(rows, cols, chans)
     pre = normed * norm_gain + norm_shift

time: 582 us -> 585 us (level)
    psum x1 -> x0, blocking collectives: 30 us -> none  [shards(): var = lax.psum(jnp.sum(centred * centred, axis=(0, 1, 3)), 'rows') / count]
    unnamed x0 -> x1, blocking collectives: none -> 30 us
where the time goes in v1:
time: 585 us; the launch traced here: 584 us
  waiting for transfers between devices  271 us (46%)
  blocking collectives  184 us (31%)
  local copies, waits for them, and re-layouts  59.1 us (10%)
  starting transfers between devices  21.4 us (4%)
  matrix products  19.1 us (3%)
  between operations  16 us (3%)
  other arithmetic  13.4 us (2%)
    psum x1, waiting for transfers between devices, shards(): lax.psum((conv_pack, small_pack, down_pack, bias_pack), ('rows', 'dp'))  271 us
    psum x1, blocking collectives, shards(): lax.psum((conv_pack, small_pack, down_pack, bias_pack), ('rows', 'dp'))  102 us
    unnamed x1, blocking collectives  30 us
    psum x1, blocking collectives, shards(): lax.psum((jnp.sum(scaled, axis=(0, 1, 3)), jnp.sum(scaled * normed_g, axi...  27.1 us
    psum x1, blocking collectives, shards(): mean = lax.psum(jnp.sum(grouped, axis=(0, 1, 3)), 'rows') / count  25.3 us
    slice x9, local copies, waits for them, and re-layouts, shards(): shifted[kh:kh + 2 * half_rows:2, kw:kw + 2 * half_cols:2]  21.5 us
  transfers between devices with their start and end apart: 7, of which 1 were waited for; matrix products, arithmetic and copies ran while one was open for 10% of the time, Pallas kernels for 0%

profile of v1, /device:TPU:1, one launch (start us, length us, event | category | flops | bytes accessed | tf_op | source)
XLA Modules:
  0.0 583.7 jit_solution(4006638615826305233)
XLA Ops:
  7.2 1.1 copy.73
  9.1 4.6 collective-permute-start
  13.7 5.5 collective-permute-start.1
  25.5 1.9 collective-permute-start.3
  28.4 1.3 dynamic-slice
  33.6 1.3 select_maximum_fusion.2
  36.0 1.8 copy.83
  37.8 1.8 copy.81
  43.4 1.2 convolution_add_fusion.15
  48.0 25.3 %psum.49 = f32[32]{0:T(128)S(1)} all-reduce(f32[32]{0:T(128)S(1)} %reduce_sum.94), channel_id=1, replica_groups=mesh['rows'=16,'dp'=32] {'rows'}, use_global_device_ids=true, to_apply=%region_2.3 | all-reduce | flops 32 | bytes 256 | tf_op jit(solution)/shard_map/psum | solution.py:64
  74.1 30.0 %all-reduce.15 = f32[512]{0:T(512)S(1)} all-reduce(f32[512]{0:T(512)S(1)} %dynamic-update-slice), channel_id=2, replica_groups=mesh['rows'=16,'dp'=32] {'rows'}, use_global_device_ids=true, to_apply=%add.15 | all-reduce | flops 512 | bytes 4096
  108.7 27.1 %all-reduce.18 = (f32[32]{0:T(128)S(1)}, f32[32]{0:T(128)S(1)}) all-reduce(f32[32]{0:T(128)S(1)} %reduce_sum.121, f32[32]{0:T(128)S(1)} %reduce_sum.118), channel_id=1, replica_groups=mesh['rows'=16,'dp'=32] {'rows'}, use_global_device_ids=true, to_apply=%region_11.12 | all-reduce | flops 64 | bytes 512 | tf_op jit(solution)/shard_map/psum | solution.py:105
  137.2 1.8 multiply_convert_fusion
  145.3 1.1 fusion.128
  146.7 101.7 %all-reduce.16 = (f32[3,128]{1,0:T(4,128)S(1)}, f32[1,256]{1,0:T(1,128)S(1)}) all-reduce(f32[3,128]{1,0:T(4,128)S(1)} %pad_maximum_fusion.12, f32[1,256]{1,0:T(1,128)S(1)} %bitcast.407), channel_id=1, replica_groups=mesh['rows'=16,'dp'=32] {'rows','dp'}, use_global_device_ids=true, to_apply=%region_16.17 | all-reduce | flops 640 | bytes 5120 | tf_op jit(solution)/shard_map/psum | solution.py:141
  249.9 4.4 collective-permute-start.2
  256.9 2.0 collective-permute-start.4
  259.0 3.0 collective-permute-start.5
  263.7 2.4 slice.255
  266.1 2.4 slice.253
  268.5 2.4 slice.251
  270.9 2.4 slice.249
  273.2 2.4 slice.247
  275.6 2.4 slice.245
  278.0 2.4 slice.243
  280.3 2.4 slice.241
  282.7 2.6 slice.257
  287.3 1.4 copy.111
  291.4 1.3 select_maximum_fusion
  303.4 270.6 %all-reduce.21.cloned.1.call-done = (f32[1152,128]{0,1:T(8,128)}, f32[1152,256]{0,1:T(8,128)}) async-done(((f32[1152,128]{0,1:T(8,128)}, f32[1152,256]{0,1:T(8,128)}), (f32[1152,128]{0,1:T(8,128)}, f32[1152,256]{0,1:T(8,128)})) %all-reduce.21.cloned.1.call-update) | async-done | bytes 1769488 | tf_op jit(solution)/shard_map/psum | solution.py:141
  574.1 1.4 constant_dynamic-slice_fusion.3
  575.5 1.4 constant_dynamic-slice_fusion.1
  (237 shorter events, 53.2 us)
Async XLA Ops:
  7.2 13.1 %copy-start = (bf16[1,1,256,256]{3,2,1,0:T(8,128)(2,1)S(1)}, bf16[1,1,256,256]{3,2,1,0:T(8,128)(2,1)}, u32[]{:S(2)}) copy-start(bf16[1,1,256,256]{3,2,1,0:T(8,128)(2,1)} %param.15) | copy-start | bytes 393220
  7.2 13.1 %copy-start.1 = (bf16[3,3,128,256]{3,2,1,0:T(8,128)(2,1)S(1)}, bf16[3,3,128,256]{3,2,1,0:T(8,128)(2,1)}, u32[]{:S(2)}) copy-start(bf16[3,3,128,256]{3,2,1,0:T(8,128)(2,1)} %param.13) | copy-start | bytes 1769476
  7.2 566.9 %all-reduce.21.cloned.1.call-start = ((), (), s32[]{:S(2)}) async-start(), calls=%async_computation | async-start | bytes 3538944 | tf_op jit(solution)/shard_map/psum | solution.py:141
  9.1 21.9 %collective-permute-start = (bf16[1,512,128]{1,2,0:T(8,128)(2,1)}, bf16[1,512,128]{1,2,0:T(8,128)(2,1)S(1)}, u32[]{:S(2)}, u32[]{:S(2)}) collective-permute-start(bf16[1,512,128]{1,2,0:T(8,128)(2,1)} %get-tuple-element.68), channel_id=1, source_target_pairs={{0,32},{32,64},{64,96},{96,128},{128,160},{160,192},{192,224},{224... | collective-permute-start | bytes 393224 | tf_op jit(solution)/shard_map/ppermute | solution.py:14
  13.7 17.3 %collective-permute-start.1 = (bf16[1,512,128]{1,2,0:T(8,128)(2,1)}, bf16[1,512,128]{1,2,0:T(8,128)(2,1)}, u32[]{:S(2)}, u32[]{:S(2)}) collective-permute-start(bf16[1,512,128]{1,2,0:T(8,128)(2,1)} %get-tuple-element.69), channel_id=1, source_target_pairs={{32,0},{64,32},{96,64},{128,96},{160,128},{192,160},{224,192},{256... | collective-permute-start | bytes 393224 | tf_op jit(solution)/shard_map/ppermute | solution.py:17
  25.5 8.1 %copy-start.5 = (f32[1,512,128]{1,2,0:T(8,128)}, f32[1,512,128]{1,2,0:T(8,128)S(1)}, u32[]{:S(2)}) copy-start(f32[1,512,128]{1,2,0:T(8,128)S(1)} %get-tuple-element.46) | copy-start | bytes 786436
  25.5 79.8 %collective-permute-start.3 = (f32[512,128]{0,1:T(8,128)}, f32[512,128]{0,1:T(8,128)}, u32[]{:S(2)}, u32[]{:S(2)}) collective-permute-start(f32[512,128]{0,1:T(8,128)} %get-tuple-element.45), channel_id=1, source_target_pairs={{32,0},{64,32},{96,64},{128,96},{160,128},{192,160},{224,192},{256... | collective-permute-start | bytes 786440 | tf_op jit(solution)/shard_map/ppermute | solution.py:25
  42.3 2.3 copy-start.9
  42.3 2.3 copy-start.22
  43.3 1.5 copy-start.20
  73.6 33.2 %copy-start.12 = (f32[1,512,32,4]{1,0,3,2:T(1,128)S(1)}, f32[1,512,32,4]{1,0,3,2:T(1,128)}, u32[]{:S(2)}) copy-start(f32[1,512,32,4]{1,0,3,2:T(1,128)} %concatenate.65) | copy-start | bytes 786436
  107.4 29.9 %copy-start.6 = (f32[1,512,128]{1,2,0:T(8,128)S(1)}, f32[1,512,128]{1,2,0:T(8,128)}, u32[]{:S(2)}) copy-start(f32[1,512,128]{1,2,0:T(8,128)} %copy-done.5) | copy-start | bytes 786436
  107.9 29.3 %copy-start.7 = (f32[2,512,128]{1,2,0:T(8,128)S(1)}, f32[2,512,128]{1,2,0:T(8,128)}, u32[]{:S(2)}) copy-start(f32[2,512,128]{1,2,0:T(8,128)} %copy.84) | copy-start | bytes 1572868
  145.3 103.7 %copy-start.4 = (bf16[1,2,512,128]{3,2,1,0:T(8,128)(2,1)S(1)}, bf16[1,2,512,128]{3,2,1,0:T(8,128)(2,1)}, u32[]{:S(2)}) copy-start(bf16[1,2,512,128]{3,2,1,0:T(8,128)(2,1)} %param.8) | copy-start | bytes 786436
  146.4 102.8 %copy-start.8 = (bf16[2,512,128]{1,2,0:T(8,128)(2,1)S(1)}, bf16[2,512,128]{1,2,0:T(8,128)(2,1)}, u32[]{:S(2)}) copy-start(bf16[2,512,128]{1,2,0:T(8,128)(2,1)} %get-tuple-element.60) | copy-start | bytes 786436
  146.4 107.9 %copy-start.35 = (f32[1,128,128]{2,1,0:T(8,128)S(1)}, f32[1,128,128]{2,1,0:T(8,128)}, u32[]{:S(2)}) copy-start(f32[1,128,128]{2,1,0:T(8,128)} %convolution_bitcast_fusion.23) | copy-start | bytes 196612
  146.5 107.9 %copy-start.36 = (f32[1,128,128]{2,1,0:T(8,128)S(1)}, f32[1,128,128]{2,1,0:T(8,128)}, u32[]{:S(2)}) copy-start(f32[1,128,128]{2,1,0:T(8,128)} %convolution_bitcast_fusion.24) | copy-start | bytes 196612
  146.7 108.8 %copy-start.33 = (f32[1,128,128]{2,1,0:T(8,128)S(1)}, f32[1,128,128]{2,1,0:T(8,128)}, u32[]{:S(2)}) copy-start(f32[1,128,128]{2,1,0:T(8,128)} %convolution_bitcast_fusion.22) | copy-start | bytes 196612
  146.7 108.8 %copy-start.34 = (f32[1,128,128]{2,1,0:T(8,128)S(1)}, f32[1,128,128]{2,1,0:T(8,128)}, u32[]{:S(2)}) copy-start(f32[1,128,128]{2,1,0:T(8,128)} %convolution_bitcast_fusion.21) | copy-start | bytes 196612
  249.9 5.8 copy-start.31
  249.9 5.8 copy-start.32
  249.9 12.7 %collective-permute-start.2 = (bf16[512,128]{0,1:T(8,128)(2,1)}, bf16[512,128]{0,1:T(8,128)(2,1)}, u32[]{:S(2)}, u32[]{:S(2)}) collective-permute-start(bf16[512,128]{0,1:T(8,128)(2,1)} %slice_bitcast_fusion.1), channel_id=1, source_target_pairs={{0,32},{32,64},{64,96},{96,128},{128,160},{160,192},{192,224},{224... | collective-permute-start | bytes 393224 | tf_op jit(solution)/shard_map/ppermute | solution.py:25
  256.9 28.5 %copy-start.2 = (bf16[3,3,128,256]{3,2,1,0:T(8,128)(2,1)S(1)}, bf16[3,3,128,256]{3,2,1,0:T(8,128)(2,1)}, u32[]{:S(2)}) copy-start(bf16[3,3,128,256]{3,2,1,0:T(8,128)(2,1)} %param.13) | copy-start | bytes 1769476
  256.9 32.4 %collective-permute-start.4 = (bf16[1,512,128]{1,2,0:T(8,128)(2,1)}, bf16[1,512,128]{1,2,0:T(8,128)(2,1)}, u32[]{:S(2)}, u32[]{:S(2)}) collective-permute-start(bf16[1,512,128]{1,2,0:T(8,128)(2,1)} %get-tuple-element.64), channel_id=1, source_target_pairs={{0,32},{32,64},{64,96},{96,128},{128,160},{160,192},{192,224},{224... | collective-permute-start | bytes 393224 | tf_op jit(solution)/shard_map/ppermute | solution.py:14
  259.0 30.4 %collective-permute-start.5 = (bf16[1,512,128]{1,2,0:T(8,128)(2,1)}, bf16[1,512,128]{1,2,0:T(8,128)(2,1)}, u32[]{:S(2)}, u32[]{:S(2)}) collective-permute-start(bf16[1,512,128]{1,2,0:T(8,128)(2,1)} %get-tuple-element.65), channel_id=1, source_target_pairs={{32,0},{64,32},{96,64},{128,96},{160,128},{192,160},{224,192},{256... | collective-permute-start | bytes 393224 | tf_op jit(solution)/shard_map/ppermute | solution.py:17
  268.5 18.2 %copy-start.23 = (bf16[1,256,128]{1,2,0:T(8,128)(2,1)}, bf16[1,256,128]{1,2,0:T(8,128)(2,1)S(1)}, u32[]{:S(2)}) copy-start(bf16[1,256,128]{1,2,0:T(8,128)(2,1)S(1)} %slice.253) | copy-start | bytes 196612
  270.8 15.7 %copy-start.25 = (bf16[1,256,128]{1,2,0:T(8,128)(2,1)}, bf16[1,256,128]{1,2,0:T(8,128)(2,1)S(1)}, u32[]{:S(2)}) copy-start(bf16[1,256,128]{1,2,0:T(8,128)(2,1)S(1)} %slice.251) | copy-start | bytes 196612
  273.2 13.1 %copy-start.27 = (bf16[1,256,128]{1,2,0:T(8,128)(2,1)}, bf16[1,256,128]{1,2,0:T(8,128)(2,1)S(1)}, u32[]{:S(2)}) copy-start(bf16[1,256,128]{1,2,0:T(8,128)(2,1)S(1)} %slice.249) | copy-start | bytes 196612
  294.0 2.2 copy-start.10
  300.0 1.9 copy-start.26
  301.0 1.5 copy-start.30
  301.0 1.5 copy-start.43
  (19 other events, 20.3 us)
Sparse Core Ops, SparseCore 0:
  300.1 273.9 all-reduce.20
